TPU v7x, 128 devices: a whole 4x4x4 slice. The times are simulated.
128 devices in a mesh: row: 8 (over y_lo, z), col: 16 (over x, y_hi, core).
Axes of the slice: x: 4, y: 4 (y_hi: 2, y_lo: 2; y = y_hi * 2 + y_lo), z: 4, core: 2. Of those that a mesh axis runs over, the one named last changes fastest.
Arguments:
- feats_one: bfloat16 [65536, 256], P(('row', 'col')), may hold values from -6 to 6
- feats_two: bfloat16 [65536, 256], P(('row', 'col')), may hold values from -6 to 6
- target_view: bfloat16 [65536, 256], P(('row', 'col')), may hold values from -6 to 6
- negatives: int32 [65536], P(('row', 'col')), may hold values from 0 to 511
- weight_one: bfloat16 [256, 256], replicated, may hold values from -0.375 to 0.375
- weight_two: bfloat16 [256, 256], replicated, may hold values from -0.375 to 0.375
- block_tiles: bfloat16 [81920, 128, 128], P(('row', 'col')), may hold values from -0.15625 to 0.15625
- tile_rows: int32 [81920], P(('row', 'col')), may hold values from 0 to 31
- tile_cols: int32 [81920], P(('row', 'col')), may hold values from 0 to 31
- block_counts: int32 [128], P(('row', 'col')), may hold values from 80 to 640, as said below
- need_rows: int32 [128, 16, 2], P(('row', 'col')), may hold values from 0 to 3, as said below
Outputs:
- grad_hidden: bfloat16 [65536, 256], P(('row', 'col'))
- grad_first: float32 [256, 256], replicated
- grad_second: float32 [256, 256], replicated
Inputs may be any that keep to these rules, and one draw needn't show every extreme that they name: `need_rows`: for each owner and source, the 2 entries are distinct. `block_counts`: live tiles of one block list.
All inputs are finite; a program needn't handle non-finite values.
Results may differ from a plain program's by a relative error of at most 0.0063.
Values may be sent and summed in bfloat16 or wider, within the bound.
No kernel may reach another device: no remote copies, remote signals or barrier semaphores. Data moves between devices by JAX's collectives and lax.ppermute only.
A program may use at most 192 MiB of HBM per device.

v0:
```python
import math
import jax
import jax.numpy as jnp
from jax import lax
from jax.sharding import PartitionSpec as P


def silu_slope(values):
    sig = jax.nn.sigmoid(values)
    return sig * (1.0 + values * (1.0 - sig))


def column_product(left, right):
    return lax.dot_general(
        left, right, (((0,), (0,)), ((), ())), preferred_element_type=jnp.float32
    )


def on_device(
    feats_one,
    feats_two,
    target_view,
    negatives,
    weight_one,
    weight_two,
    block_tiles,
    tile_rows,
    tile_cols,
    block_counts,
    need_rows,
):
    node_dev, features = feats_two.shape
    capacity, tile_size = (block_tiles.shape[0], block_tiles.shape[1])
    sources = lax.axis_size("col")
    row_group = lax.axis_size("row")
    tiles_dev = node_dev // tile_size
    slot_count = need_rows.shape[2]
    col_count = row_group * tiles_dev
    inverse_root = 1.0 / math.sqrt(features)
    weight_norm = 1.0 / math.sqrt(node_dev * row_group * sources)
    pre_two = jnp.dot(feats_two, weight_two, preferred_element_type=jnp.float32)
    hidden = jax.nn.silu(pre_two)
    partner_rows = hidden[negatives]
    target_full = target_view.astype(jnp.float32)
    s_pos = jnp.sum(hidden * target_full, axis=-1) * inverse_root
    s_neg = jnp.sum(hidden * partner_rows, axis=-1) * inverse_root
    prob_pos = jax.nn.sigmoid(-s_pos)
    prob_neg = jax.nn.sigmoid(s_neg)
    grad_out = -prob_pos[:, None] * target_full + prob_neg[:, None] * partner_rows
    grad_out = grad_out + jax.ops.segment_sum(
        prob_neg[:, None] * hidden, negatives, num_segments=node_dev
    )
    dpre_two = (grad_out * silu_slope(pre_two)).astype(jnp.bfloat16)
    grad_second = column_product(feats_two, dpre_two)
    grad_second = lax.psum(grad_second, ("row", "col"))
    message = lax.dot_general(
        dpre_two, weight_two, (((1,), (1,)), ((), ())), preferred_element_type=jnp.float32
    ).astype(jnp.bfloat16)
    gathered = lax.all_gather(message, "col", axis=0, tiled=True)
    buffer_tiles = gathered.reshape(sources * tiles_dev, tile_size, features)
    need_flat = need_rows[0].reshape(-1)
    slot_ids = jnp.arange(sources * slot_count, dtype=jnp.int32)
    local_tile = jnp.sum(
        jnp.where(tile_rows[:, None] == slot_ids[None, :], need_flat[None, :], 0), axis=1
    )
    row_tile = tile_rows // slot_count * tiles_dev + local_tile
    block_len = 128
    rounds = capacity // block_len
    live = (jnp.arange(capacity, dtype=jnp.int32) < block_counts[0]).astype(jnp.float32)
    column_ids = jnp.arange(col_count, dtype=jnp.int32)

    def add_block(summed_tiles, pieces):
        tile_part, row_part, col_part, live_part = pieces
        gathered_rows = buffer_tiles[row_part]
        contrib = jnp.einsum(
            "ktu,ktf->kuf", tile_part, gathered_rows, preferred_element_type=jnp.float32
        )
        selector = jnp.where(col_part[:, None] == column_ids[None, :], live_part[:, None], 0.0)
        placed = jnp.einsum(
            "kc,kuf->cuf",
            selector,
            contrib,
            precision=lax.Precision.HIGHEST,
            preferred_element_type=jnp.float32,
        )
        return (summed_tiles + placed, None)

    start_tiles = jnp.zeros((col_count, tile_size, features), jnp.float32)
    summed_tiles, _ = lax.scan(
        add_block,
        start_tiles,
        (
            block_tiles.reshape(rounds, block_len, tile_size, tile_size),
            row_tile.reshape(rounds, block_len),
            tile_cols.reshape(rounds, block_len),
            live.reshape(rounds, block_len),
        ),
    )
    column_total = lax.psum_scatter(
        summed_tiles.reshape(col_count * tile_size, features),
        "row",
        scatter_dimension=0,
        tiled=True,
    )
    grad_hidden = column_total.astype(jnp.bfloat16)
    pre_one = jnp.dot(feats_one, weight_one, preferred_element_type=jnp.float32)
    dpre_one = (grad_hidden.astype(jnp.float32) * silu_slope(pre_one)).astype(jnp.bfloat16)
    grad_first = column_product(feats_one, dpre_one)
    grad_first = lax.psum(grad_first, ("row", "col"))
    return (grad_hidden, grad_first * weight_norm, grad_second * weight_norm)


def solution(mesh):
    return jax.shard_map(
        on_device,
        mesh=mesh,
        in_specs=(
            P(("row", "col"), None),
            P(("row", "col"), None),
            P(("row", "col"), None),
            P(("row", "col")),
            P(),
            P(),
            P(("row", "col"), None, None),
            P(("row", "col")),
            P(("row", "col")),
            P(("row", "col")),
            P(("row", "col"), None, None),
        ),
        out_specs=(P(("row", "col"), None), P(), P()),
        check_vma=False,
    )
```

profile of v0, /device:TPU:1, one launch (start us, length us, event | category | flops | bytes accessed | tf_op | source)
XLA Modules:
  0.0 544.5 jit_solution(12721467284938459450)
XLA Ops:
  7.2 1.0 copy-done
  8.2 1.2 fusion.22
  9.5 0.2 copy.43
  9.7 0.7 compare_select_fusion.1
  10.4 1.6 gather_fusion.1
  11.9 0.2 copy.44
  12.5 0.2 broadcast_multiply_fusion
  12.6 0.2 copy.46
  12.8 0.2 copy.47
  13.1 3.5 scatter_fusion
  16.6 0.2 copy.48
  16.8 0.2 multiply_convert_fusion.1
  17.0 1.0 convolution_convert_fusion
  18.1 27.9 %copy.40 = bf16[640,128,128]{1,2,0:T(8,128)(2,1)} copy(bf16[640,128,128]{2,1,0:T(8,128)(2,1)} %param.19) | data formatting | bytes 41943040 | tf_op args[6]
  47.0 30.8 %all-gather.2.cloned.1.call-done = bf16[8192,256]{1,0:T(8,128)(2,1)} async-done(((bf16[512,256]{1,0:T(8,128)(2,1)}), bf16[8192,256]{1,0:T(8,128)(2,1)}) %all-gather.2.cloned.1.call-update) | async-done | bytes 4194320 | tf_op jit(solution)/shard_map/all_gather | solution.py:59
  77.8 241.0 %while.11 = (s32[]{:T(128)}, f32[32,128,256]{2,0,1:T(8,128)}, s32[5,128]{1,0:T(8,128)}, f32[5,128]{1,0:T(8,128)S(1)}, bf16[5,128,128,128]{2,3,1,0:T(8,128)(2,1)}...) while((s32[]{:T(128)}, f32[32,128,256]{2,0,1:T(8,128)}, ...), condition=%wide.region_5.6_spmd.clone, body=%wide.region_4.5_spmd.clone.sunk | while | flops 2686461440 | bytes 71313008 | solution.py:89
  77.8 8.7 %gather_fusion = bf16[128,128,256]{2,1,0:T(8,128)(2,1)} fusion(bf16[64,128,256]{2,1,0:T(8,128)(2,1)} %get-tuple-element.172, s32[1024]{0:T(1024)S(1)} %pad_clamp_fusion.3), kind=kCustom, calls=%fused_computation.clone.clone.1 | custom fusion | bytes 16777728 | tf_op jit(solution)/shard_map/while/body/eval_jaxpr/gather | solution.py:74
  86.5 12.8 %fusion.55 = f32[128,128,256]{2,1,0:T(8,128)} fusion(bf16[128,128,256]{2,1,0:T(8,128)(2,1)} %gather_fusion, bf16[5,128,128,128]{2,3,1,0:T(8,128)(2,1)} %get-tuple-element.170, s32[]{:T(128)} %get-tuple-element.157), kind=kOutput, calls=%fused_computation.6.clone.1 | convolution fusion | flops 1073741824 | bytes 29360640 | tf_op jit(solution)/shard_map/while/body/eval_jaxpr/ktu,ktf->kuf/dot_general | solution.py:75
  99.4 0.7 fusion.57
  100.0 25.4 %select_add_fusion.2 = f32[32,128,256]{2,0,1:T(8,128)} fusion(f32[32,128,256]{2,0,1:T(8,128)} %get-tuple-element.158, pred[]{:T(512)S(6)} %compare.5, f32[128,128,256]{2,1,0:T(8,128)} %fusion.55, f32[128]{0:T(128)S(1)} %fusion.56, s32[128]{0:T(128)S(1)} %fusion.57), kind=kOutput, calls=%fused_computation.8.clone.1 | convolution fusion | flops 1612718080 | bytes 25166848 | tf_op jit(solution)/shard_map/while/body/eval_jaxpr/kc,kuf->cuf/dot_general | solution.py:79
  125.5 8.7 %gather_fusion = bf16[128,128,256]{2,1,0:T(8,128)(2,1)} fusion(bf16[64,128,256]{2,1,0:T(8,128)(2,1)} %get-tuple-element.172, s32[1024]{0:T(1024)S(1)} %pad_clamp_fusion.3), kind=kCustom, calls=%fused_computation.clone.clone.1 | custom fusion | bytes 16777728 | tf_op jit(solution)/shard_map/while/body/eval_jaxpr/gather | solution.py:74
  134.2 12.8 %fusion.55 = f32[128,128,256]{2,1,0:T(8,128)} fusion(bf16[128,128,256]{2,1,0:T(8,128)(2,1)} %gather_fusion, bf16[5,128,128,128]{2,3,1,0:T(8,128)(2,1)} %get-tuple-element.170, s32[]{:T(128)} %get-tuple-element.157), kind=kOutput, calls=%fused_computation.6.clone.1 | convolution fusion | flops 1073741824 | bytes 29360640 | tf_op jit(solution)/shard_map/while/body/eval_jaxpr/ktu,ktf->kuf/dot_general | solution.py:75
  147.1 0.7 fusion.57
  147.8 26.0 %select_add_fusion.2 = f32[32,128,256]{2,0,1:T(8,128)} fusion(f32[32,128,256]{2,0,1:T(8,128)} %get-tuple-element.158, pred[]{:T(512)S(6)} %compare.5, f32[128,128,256]{2,1,0:T(8,128)} %fusion.55, f32[128]{0:T(128)S(1)} %fusion.56, s32[128]{0:T(128)S(1)} %fusion.57), kind=kOutput, calls=%fused_computation.8.clone.1 | convolution fusion | flops 1612718080 | bytes 25166848 | tf_op jit(solution)/shard_map/while/body/eval_jaxpr/kc,kuf->cuf/dot_general | solution.py:79
  173.8 8.7 %gather_fusion = bf16[128,128,256]{2,1,0:T(8,128)(2,1)} fusion(bf16[64,128,256]{2,1,0:T(8,128)(2,1)} %get-tuple-element.172, s32[1024]{0:T(1024)S(1)} %pad_clamp_fusion.3), kind=kCustom, calls=%fused_computation.clone.clone.1 | custom fusion | bytes 16777728 | tf_op jit(solution)/shard_map/while/body/eval_jaxpr/gather | solution.py:74
  182.6 12.8 %fusion.55 = f32[128,128,256]{2,1,0:T(8,128)} fusion(bf16[128,128,256]{2,1,0:T(8,128)(2,1)} %gather_fusion, bf16[5,128,128,128]{2,3,1,0:T(8,128)(2,1)} %get-tuple-element.170, s32[]{:T(128)} %get-tuple-element.157), kind=kOutput, calls=%fused_computation.6.clone.1 | convolution fusion | flops 1073741824 | bytes 29360640 | tf_op jit(solution)/shard_map/while/body/eval_jaxpr/ktu,ktf->kuf/dot_general | solution.py:75
  195.4 0.7 fusion.57
  196.1 26.0 %select_add_fusion.2 = f32[32,128,256]{2,0,1:T(8,128)} fusion(f32[32,128,256]{2,0,1:T(8,128)} %get-tuple-element.158, pred[]{:T(512)S(6)} %compare.5, f32[128,128,256]{2,1,0:T(8,128)} %fusion.55, f32[128]{0:T(128)S(1)} %fusion.56, s32[128]{0:T(128)S(1)} %fusion.57), kind=kOutput, calls=%fused_computation.8.clone.1 | convolution fusion | flops 1612718080 | bytes 25166848 | tf_op jit(solution)/shard_map/while/body/eval_jaxpr/kc,kuf->cuf/dot_general | solution.py:79
  222.2 8.8 %gather_fusion = bf16[128,128,256]{2,1,0:T(8,128)(2,1)} fusion(bf16[64,128,256]{2,1,0:T(8,128)(2,1)} %get-tuple-element.172, s32[1024]{0:T(1024)S(1)} %pad_clamp_fusion.3), kind=kCustom, calls=%fused_computation.clone.clone.1 | custom fusion | bytes 16777728 | tf_op jit(solution)/shard_map/while/body/eval_jaxpr/gather | solution.py:74
  230.9 12.8 %fusion.55 = f32[128,128,256]{2,1,0:T(8,128)} fusion(bf16[128,128,256]{2,1,0:T(8,128)(2,1)} %gather_fusion, bf16[5,128,128,128]{2,3,1,0:T(8,128)(2,1)} %get-tuple-element.170, s32[]{:T(128)} %get-tuple-element.157), kind=kOutput, calls=%fused_computation.6.clone.1 | convolution fusion | flops 1073741824 | bytes 29360640 | tf_op jit(solution)/shard_map/while/body/eval_jaxpr/ktu,ktf->kuf/dot_general | solution.py:75
  243.7 0.7 fusion.57
  244.4 26.0 %select_add_fusion.2 = f32[32,128,256]{2,0,1:T(8,128)} fusion(f32[32,128,256]{2,0,1:T(8,128)} %get-tuple-element.158, pred[]{:T(512)S(6)} %compare.5, f32[128,128,256]{2,1,0:T(8,128)} %fusion.55, f32[128]{0:T(128)S(1)} %fusion.56, s32[128]{0:T(128)S(1)} %fusion.57), kind=kOutput, calls=%fused_computation.8.clone.1 | convolution fusion | flops 1612718080 | bytes 25166848 | tf_op jit(solution)/shard_map/while/body/eval_jaxpr/kc,kuf->cuf/dot_general | solution.py:79
  270.5 8.7 %gather_fusion = bf16[128,128,256]{2,1,0:T(8,128)(2,1)} fusion(bf16[64,128,256]{2,1,0:T(8,128)(2,1)} %get-tuple-element.172, s32[1024]{0:T(1024)S(1)} %pad_clamp_fusion.3), kind=kCustom, calls=%fused_computation.clone.clone.1 | custom fusion | bytes 16777728 | tf_op jit(solution)/shard_map/while/body/eval_jaxpr/gather | solution.py:74
  279.2 12.8 %fusion.55 = f32[128,128,256]{2,1,0:T(8,128)} fusion(bf16[128,128,256]{2,1,0:T(8,128)(2,1)} %gather_fusion, bf16[5,128,128,128]{2,3,1,0:T(8,128)(2,1)} %get-tuple-element.170, s32[]{:T(128)} %get-tuple-element.157), kind=kOutput, calls=%fused_computation.6.clone.1 | convolution fusion | flops 1073741824 | bytes 29360640 | tf_op jit(solution)/shard_map/while/body/eval_jaxpr/ktu,ktf->kuf/dot_general | solution.py:75
  292.1 0.7 fusion.57
  292.8 26.0 %select_add_fusion.2 = f32[32,128,256]{2,0,1:T(8,128)} fusion(f32[32,128,256]{2,0,1:T(8,128)} %get-tuple-element.158, pred[]{:T(512)S(6)} %compare.5, f32[128,128,256]{2,1,0:T(8,128)} %fusion.55, f32[128]{0:T(128)S(1)} %fusion.56, s32[128]{0:T(128)S(1)} %fusion.57), kind=kOutput, calls=%fused_computation.8.clone.1 | convolution fusion | flops 1612718080 | bytes 25166848 | tf_op jit(solution)/shard_map/while/body/eval_jaxpr/kc,kuf->cuf/dot_general | solution.py:79
  318.8 5.9 %copy.49 = f32[32,128,256]{1,0,2:T(8,128)} copy(f32[32,128,256]{2,0,1:T(8,128)} %get-tuple-element.45) | data formatting | bytes 8388608 | tf_op jit(solution)/shard_map/while | solution.py:89
  324.8 8.0 %copy.62 = f32[32,8,32,128]{3,1,2,0:T(8,128)} copy(f32[32,8,32,128]{3,2,1,0:T(8,128)} %bitcast.62) | data formatting | bytes 8388608
  332.8 0.9 convolution_bitcast_fusion
  333.8 50.9 %reduce-scatter.2.cloned.1.call-done = f32[512,256]{0,1:T(8,128)} async-done(((f32[4096,256]{0,1:T(8,128)}), f32[512,256]{0,1:T(8,128)}) %reduce-scatter.2.cloned.1.call-update) | async-done | bytes 524304 | tf_op jit(solution)/shard_map/reduce_scatter | solution.py:99
  384.7 1.1 convert_element_type.26
  385.8 1.2 convolution_bitcast_fusion.1
  387.0 0.8 copy.52
  387.9 146.5 %all-reduce.3.cloned.1.call-done = (f32[256,256]{0,1:T(8,128)}, f32[256,256]{0,1:T(8,128)}) async-done(((f32[256,256]{0,1:T(8,128)}, f32[256,256]{0,1:T(8,128)}), (f32[256,256]{0,1:T(8,128)}, f32[256,256]{0,1:T(8,128)})) %all-reduce.3.cloned.1.call-update) | async-done | bytes 524304 | tf_op jit(solution)/shard_map/psum | solution.py:109
  534.4 1.0 broadcast_multiply_fusion.2
  535.3 0.8 copy.53
  536.2 1.0 broadcast_multiply_fusion.1
  537.1 0.8 copy.54
  (46 shorter events, 0.9 us)
Async XLA Ops:
  7.2 1.0 copy-start
  7.2 5.9 %copy-start.4 = (s32[512]{0:T(512)S(1)}, s32[512]{0:T(512)}, u32[]{:S(2)}) copy-start(s32[512]{0:T(512)} %param.16) | copy-start | bytes 6148
  7.2 4.9 copy-start.1
  7.2 70.6 %all-gather.2.cloned.1.call-start = ((), (), s32[]{:S(2)}) async-start(), calls=%async_computation.1 | async-start | bytes 4456448 | tf_op jit(solution)/shard_map/all_gather | solution.py:59
  12.3 4.7 copy-start.2
  18.0 366.7 %reduce-scatter.2.cloned.1.call-start = ((), (), s32[]{:S(2)}) async-start(), calls=%async_computation.2 | async-start | bytes 4718592 | tf_op jit(solution)/shard_map/reduce_scatter | solution.py:99
  18.1 27.9 %copy-start.5 = (s32[1,16,2]{1,2,0:T(2,128)S(1)}, s32[1,16,2]{1,2,0:T(2,128)}, u32[]{:S(2)}) copy-start(s32[1,16,2]{1,2,0:T(2,128)} %param.23) | copy-start | bytes 388
  18.1 28.8 %copy-start.3 = (s32[640]{0:T(1024)S(1)}, s32[640]{0:T(1024)}, u32[]{:S(2)}) copy-start(s32[640]{0:T(1024)} %param.20) | copy-start | bytes 7684
  324.8 61.0 %copy-start.6 = (bf16[512,256]{1,0:T(8,128)(2,1)S(1)}, bf16[512,256]{1,0:T(8,128)(2,1)}, u32[]{:S(2)}) copy-start(bf16[512,256]{1,0:T(8,128)(2,1)} %param.13) | copy-start | bytes 786436
  324.8 61.0 %copy-start.7 = (bf16[256,256]{1,0:T(8,128)(2,1)S(1)}, bf16[256,256]{1,0:T(8,128)(2,1)}, u32[]{:S(2)}) copy-start(bf16[256,256]{1,0:T(8,128)(2,1)} %param.17) | copy-start | bytes 393220
  332.8 201.6 %all-reduce.3.cloned.1.call-start = ((), (), s32[]{:S(2)}) async-start(), calls=%async_computation.3 | async-start | bytes 1048576 | tf_op jit(solution)/shard_map/psum | solution.py:109
Sparse Core Ops, SparseCore 0:
  18.2 59.5 all-gather.1
  332.9 51.7 reduce-scatter.1
  390.2 144.0 all-reduce.2
where the time goes:
time: 546 us; the launch traced here: 544 us
  waiting for transfers between devices  228 us (42%)
  matrix products  198 us (36%)
  local copies, waits for them, and re-layouts  95.4 us (17%)
  between operations  14.6 us (3%)
  other arithmetic  7.94 us (1%)
    psum x1, waiting for transfers between devices, on_device(): grad_first = lax.psum(grad_first, ('row', 'col'))  146 us
    dot_general x5, matrix products, add_block(): jnp.einsum('kc,kuf->cuf', selector, contrib, precision=lax.Precision.HIGH...  130 us
    dot_general x5, matrix products, add_block(): jnp.einsum('ktu,ktf->kuf', tile_part, gathered_rows, preferred_element_ty...  64.1 us
    reduce_scatter x1, waiting for transfers between devices, on_device(): lax.psum_scatter(summed_tiles.reshape(col_count * tile_size, features), '...  50.9 us
    gather x5, local copies, waits for them, and re-layouts, add_block(): gathered_rows = buffer_tiles[row_part]  43.7 us
    unnamed x23, local copies, waits for them, and re-layouts  39.7 us
    all_gather x1, waiting for transfers between devices, on_device(): gathered = lax.all_gather(message, 'col', axis=0, tiled=True)  30.8 us
  transfers between devices with their start and end apart: 3, of which 3 were waited for; matrix products, arithmetic and copies ran while one was open for 6% of the time, Pallas kernels for 0%

commit v1 on v0

--- a/solution.py
+++ b/solution.py
@@ -56,7 +56,12 @@
     message = lax.dot_general(
         dpre_two, weight_two, (((1,), (1,)), ((), ())), preferred_element_type=jnp.float32
     ).astype(jnp.bfloat16)
-    gathered = lax.all_gather(message, "col", axis=0, tiled=True)
+    gathered = jnp.concatenate(
+        lax.all_to_all(
+            jnp.stack([message] * lax.axis_size("col"), axis=0), "col", split_axis=0, concat_axis=0
+        ),
+        axis=0,
+    )
     buffer_tiles = gathered.reshape(sources * tiles_dev, tile_size, features)
     need_flat = need_rows[0].reshape(-1)
     slot_ids = jnp.arange(sources * slot_count, dtype=jnp.int32)

time: 546 us -> 559 us (1.024)
  starting transfers between devices: 0.12 us -> 8.52 us
    all_gather x1 -> x0, waiting for transfers between devices: 30.8 us -> none  [on_device(): gathered = lax.all_gather(message, 'col', axis=0, tiled=True)]
    all_to_all x0 -> x1, waiting for transfers between devices: none -> 23.8 us  [on_device(): lax.all_to_all(jnp.stack([message] * lax.axis_size('col'), axis=0), 'col'...]
    reduce_scatter x1, waiting for transfers between devices: 50.9 us -> 60.2 us  [on_device(): lax.psum_scatter(summed_tiles.reshape(col_count * tile_size, features), '...]
    all_to_all x0 -> x1, starting transfers between devices: none -> 8.44 us  [on_device(): lax.all_to_all(jnp.stack([message] * lax.axis_size('col'), axis=0), 'col'...]
    unnamed x23 -> x27, local copies, waits for them, and re-layouts: 39.7 us -> 40.4 us
  transfers between devices with their start and end apart: 3 -> 3, of which waited for: 3 -> 3; matrix products, arithmetic and copies ran while one was open for 6% -> 5% of each run, Pallas kernels for 0% -> 0%
where the time goes in v1:
time: 559 us; the launch traced here: 558 us
  waiting for transfers between devices  231 us (41%)
  matrix products  197 us (35%)
  local copies, waits for them, and re-layouts  98.5 us (18%)
  between operations  14.9 us (3%)
  starting transfers between devices  8.52 us (2%)
  other arithmetic  7.94 us (1%)
    psum x1, waiting for transfers between devices, on_device(): grad_first = lax.psum(grad_first, ('row', 'col'))  146 us
    dot_general x5, matrix products, add_block(): jnp.einsum('kc,kuf->cuf', selector, contrib, precision=lax.Precision.HIGH...  130 us
    dot_general x5, matrix products, add_block(): jnp.einsum('ktu,ktf->kuf', tile_part, gathered_rows, preferred_element_ty...  64.2 us
    reduce_scatter x1, waiting for transfers between devices, on_device(): lax.psum_scatter(summed_tiles.reshape(col_count * tile_size, features), '...  60.2 us
    gather x5, local copies, waits for them, and re-layouts, add_block(): gathered_rows = buffer_tiles[row_part]  43.7 us
    unnamed x27, local copies, waits for them, and re-layouts  40.4 us
    all_to_all x1, waiting for transfers between devices, on_device(): lax.all_to_all(jnp.stack([message] * lax.axis_size('col'), axis=0), 'col'...  23.8 us
  transfers between devices with their start and end apart: 3, of which 3 were waited for; matrix products, arithmetic and copies ran while one was open for 5% of the time, Pallas kernels for 0%

profile of v1, /device:TPU:1, one launch (start us, length us, event | category | flops | bytes accessed | tf_op | source)
XLA Modules:
  0.0 558.0 jit_solution(15808698724482401553)
XLA Ops:
  7.2 1.0 copy-done
  8.2 1.2 fusion.22
  9.7 0.7 compare_select_fusion.1
  10.4 1.6 gather_fusion.1
  11.9 0.2 copy.44
  12.6 0.2 copy.46
  13.1 3.5 scatter_fusion
  16.6 0.2 copy.48
  16.8 0.2 multiply_convert_fusion.1
  17.0 0.7 copy-done.1
  17.7 0.3 convolution_convert_fusion
  18.0 2.4 stack.2
  20.4 8.4 %all-to-all-start = ((bf16[16,512,256]{2,1,0:T(8,128)(2,1)}), bf16[16,512,256]{2,1,0:T(8,128)(2,1)}, u32[]{:S(2)}, u32[]{:S(2)}) async-start(bf16[16,512,256]{2,1,0:T(8,128)(2,1)} %stack.2), calls=%async_computation | async-start | bytes 8388608 | tf_op jit(solution)/shard_map/all_to_all | solution.py:60
  28.9 27.9 %copy.40 = bf16[640,128,128]{1,2,0:T(8,128)(2,1)} copy(bf16[640,128,128]{2,1,0:T(8,128)(2,1)} %param.19) | data formatting | bytes 41943040 | tf_op args[6]
  57.7 23.8 %all-to-all-done = bf16[16,512,256]{2,1,0:T(8,128)(2,1)} async-done(((bf16[16,512,256]{2,1,0:T(8,128)(2,1)}), bf16[16,512,256]{2,1,0:T(8,128)(2,1)}, u32[]{:S(2)}, u32[]{:S(2)}) %all-to-all-start) | async-done | bytes 4194336 | tf_op jit(solution)/shard_map/all_to_all | solution.py:60
  81.6 241.1 %while.11 = (s32[]{:T(128)}, f32[32,128,256]{2,0,1:T(8,128)}, s32[5,128]{1,0:T(8,128)}, f32[5,128]{1,0:T(8,128)S(1)}, bf16[5,128,128,128]{2,3,1,0:T(8,128)(2,1)}...) while((s32[]{:T(128)}, f32[32,128,256]{2,0,1:T(8,128)}, ...), condition=%wide.region_5.6_spmd.clone, body=%wide.region_4.5_spmd.clone.sunk | while | flops 2686461440 | bytes 71313008 | solution.py:94
  81.6 8.7 %gather_fusion = bf16[128,128,256]{2,1,0:T(8,128)(2,1)} fusion(bf16[64,128,256]{2,1,0:T(8,128)(2,1)} %get-tuple-element.172, s32[1024]{0:T(1024)S(1)} %pad_clamp_fusion.3), kind=kCustom, calls=%fused_computation.clone.clone.1 | custom fusion | bytes 16777728 | tf_op jit(solution)/shard_map/while/body/eval_jaxpr/gather | solution.py:79
  90.3 12.8 %fusion.55 = f32[128,128,256]{2,1,0:T(8,128)} fusion(bf16[128,128,256]{2,1,0:T(8,128)(2,1)} %gather_fusion, bf16[5,128,128,128]{2,3,1,0:T(8,128)(2,1)} %get-tuple-element.170, s32[]{:T(128)} %get-tuple-element.157), kind=kOutput, calls=%fused_computation.6.clone.1 | convolution fusion | flops 1073741824 | bytes 29360640 | tf_op jit(solution)/shard_map/while/body/eval_jaxpr/ktu,ktf->kuf/dot_general | solution.py:80
  103.1 0.7 fusion.57
  103.8 25.4 %select_add_fusion.2 = f32[32,128,256]{2,0,1:T(8,128)} fusion(f32[32,128,256]{2,0,1:T(8,128)} %get-tuple-element.158, pred[]{:T(512)S(6)} %compare.5, f32[128,128,256]{2,1,0:T(8,128)} %fusion.55, f32[128]{0:T(128)S(1)} %fusion.56, s32[128]{0:T(128)S(1)} %fusion.57), kind=kOutput, calls=%fused_computation.8.clone.1 | convolution fusion | flops 1612718080 | bytes 25166848 | tf_op jit(solution)/shard_map/while/body/eval_jaxpr/kc,kuf->cuf/dot_general | solution.py:84
  129.3 8.7 %gather_fusion = bf16[128,128,256]{2,1,0:T(8,128)(2,1)} fusion(bf16[64,128,256]{2,1,0:T(8,128)(2,1)} %get-tuple-element.172, s32[1024]{0:T(1024)S(1)} %pad_clamp_fusion.3), kind=kCustom, calls=%fused_computation.clone.clone.1 | custom fusion | bytes 16777728 | tf_op jit(solution)/shard_map/while/body/eval_jaxpr/gather | solution.py:79
  138.0 12.8 %fusion.55 = f32[128,128,256]{2,1,0:T(8,128)} fusion(bf16[128,128,256]{2,1,0:T(8,128)(2,1)} %gather_fusion, bf16[5,128,128,128]{2,3,1,0:T(8,128)(2,1)} %get-tuple-element.170, s32[]{:T(128)} %get-tuple-element.157), kind=kOutput, calls=%fused_computation.6.clone.1 | convolution fusion | flops 1073741824 | bytes 29360640 | tf_op jit(solution)/shard_map/while/body/eval_jaxpr/ktu,ktf->kuf/dot_general | solution.py:80
  150.9 0.7 fusion.57
  151.6 26.0 %select_add_fusion.2 = f32[32,128,256]{2,0,1:T(8,128)} fusion(f32[32,128,256]{2,0,1:T(8,128)} %get-tuple-element.158, pred[]{:T(512)S(6)} %compare.5, f32[128,128,256]{2,1,0:T(8,128)} %fusion.55, f32[128]{0:T(128)S(1)} %fusion.56, s32[128]{0:T(128)S(1)} %fusion.57), kind=kOutput, calls=%fused_computation.8.clone.1 | convolution fusion | flops 1612718080 | bytes 25166848 | tf_op jit(solution)/shard_map/while/body/eval_jaxpr/kc,kuf->cuf/dot_general | solution.py:84
  177.6 8.7 %gather_fusion = bf16[128,128,256]{2,1,0:T(8,128)(2,1)} fusion(bf16[64,128,256]{2,1,0:T(8,128)(2,1)} %get-tuple-element.172, s32[1024]{0:T(1024)S(1)} %pad_clamp_fusion.3), kind=kCustom, calls=%fused_computation.clone.clone.1 | custom fusion | bytes 16777728 | tf_op jit(solution)/shard_map/while/body/eval_jaxpr/gather | solution.py:79
  186.4 12.8 %fusion.55 = f32[128,128,256]{2,1,0:T(8,128)} fusion(bf16[128,128,256]{2,1,0:T(8,128)(2,1)} %gather_fusion, bf16[5,128,128,128]{2,3,1,0:T(8,128)(2,1)} %get-tuple-element.170, s32[]{:T(128)} %get-tuple-element.157), kind=kOutput, calls=%fused_computation.6.clone.1 | convolution fusion | flops 1073741824 | bytes 29360640 | tf_op jit(solution)/shard_map/while/body/eval_jaxpr/ktu,ktf->kuf/dot_general | solution.py:80
  199.2 0.7 fusion.57
  199.9 26.0 %select_add_fusion.2 = f32[32,128,256]{2,0,1:T(8,128)} fusion(f32[32,128,256]{2,0,1:T(8,128)} %get-tuple-element.158, pred[]{:T(512)S(6)} %compare.5, f32[128,128,256]{2,1,0:T(8,128)} %fusion.55, f32[128]{0:T(128)S(1)} %fusion.56, s32[128]{0:T(128)S(1)} %fusion.57), kind=kOutput, calls=%fused_computation.8.clone.1 | convolution fusion | flops 1612718080 | bytes 25166848 | tf_op jit(solution)/shard_map/while/body/eval_jaxpr/kc,kuf->cuf/dot_general | solution.py:84
  226.0 8.7 %gather_fusion = bf16[128,128,256]{2,1,0:T(8,128)(2,1)} fusion(bf16[64,128,256]{2,1,0:T(8,128)(2,1)} %get-tuple-element.172, s32[1024]{0:T(1024)S(1)} %pad_clamp_fusion.3), kind=kCustom, calls=%fused_computation.clone.clone.1 | custom fusion | bytes 16777728 | tf_op jit(solution)/shard_map/while/body/eval_jaxpr/gather | solution.py:79
  234.7 12.8 %fusion.55 = f32[128,128,256]{2,1,0:T(8,128)} fusion(bf16[128,128,256]{2,1,0:T(8,128)(2,1)} %gather_fusion, bf16[5,128,128,128]{2,3,1,0:T(8,128)(2,1)} %get-tuple-element.170, s32[]{:T(128)} %get-tuple-element.157), kind=kOutput, calls=%fused_computation.6.clone.1 | convolution fusion | flops 1073741824 | bytes 29360640 | tf_op jit(solution)/shard_map/while/body/eval_jaxpr/ktu,ktf->kuf/dot_general | solution.py:80
  247.6 0.7 fusion.57
  248.3 26.0 %select_add_fusion.2 = f32[32,128,256]{2,0,1:T(8,128)} fusion(f32[32,128,256]{2,0,1:T(8,128)} %get-tuple-element.158, pred[]{:T(512)S(6)} %compare.5, f32[128,128,256]{2,1,0:T(8,128)} %fusion.55, f32[128]{0:T(128)S(1)} %fusion.56, s32[128]{0:T(128)S(1)} %fusion.57), kind=kOutput, calls=%fused_computation.8.clone.1 | convolution fusion | flops 1612718080 | bytes 25166848 | tf_op jit(solution)/shard_map/while/body/eval_jaxpr/kc,kuf->cuf/dot_general | solution.py:84
  274.3 8.7 %gather_fusion = bf16[128,128,256]{2,1,0:T(8,128)(2,1)} fusion(bf16[64,128,256]{2,1,0:T(8,128)(2,1)} %get-tuple-element.172, s32[1024]{0:T(1024)S(1)} %pad_clamp_fusion.3), kind=kCustom, calls=%fused_computation.clone.clone.1 | custom fusion | bytes 16777728 | tf_op jit(solution)/shard_map/while/body/eval_jaxpr/gather | solution.py:79
  283.1 12.8 %fusion.55 = f32[128,128,256]{2,1,0:T(8,128)} fusion(bf16[128,128,256]{2,1,0:T(8,128)(2,1)} %gather_fusion, bf16[5,128,128,128]{2,3,1,0:T(8,128)(2,1)} %get-tuple-element.170, s32[]{:T(128)} %get-tuple-element.157), kind=kOutput, calls=%fused_computation.6.clone.1 | convolution fusion | flops 1073741824 | bytes 29360640 | tf_op jit(solution)/shard_map/while/body/eval_jaxpr/ktu,ktf->kuf/dot_general | solution.py:80
  295.9 0.7 fusion.57
  296.6 26.0 %select_add_fusion.2 = f32[32,128,256]{2,0,1:T(8,128)} fusion(f32[32,128,256]{2,0,1:T(8,128)} %get-tuple-element.158, pred[]{:T(512)S(6)} %compare.5, f32[128,128,256]{2,1,0:T(8,128)} %fusion.55, f32[128]{0:T(128)S(1)} %fusion.56, s32[128]{0:T(128)S(1)} %fusion.57), kind=kOutput, calls=%fused_computation.8.clone.1 | convolution fusion | flops 1612718080 | bytes 25166848 | tf_op jit(solution)/shard_map/while/body/eval_jaxpr/kc,kuf->cuf/dot_general | solution.py:84
  322.6 5.9 %copy.49 = f32[32,128,256]{1,0,2:T(8,128)} copy(f32[32,128,256]{2,0,1:T(8,128)} %get-tuple-element.45) | data formatting | bytes 8388608 | tf_op jit(solution)/shard_map/while | solution.py:94
  328.6 8.0 %copy.62 = f32[32,8,32,128]{3,1,2,0:T(8,128)} copy(f32[32,8,32,128]{3,2,1,0:T(8,128)} %bitcast.61) | data formatting | bytes 8388608
  336.7 0.9 convolution_bitcast_fusion
  337.6 60.2 %reduce-scatter.2.cloned.1.call-done = f32[512,256]{0,1:T(8,128)} async-done(((f32[4096,256]{0,1:T(8,128)}), f32[512,256]{0,1:T(8,128)}) %reduce-scatter.2.cloned.1.call-update) | async-done | bytes 524304 | tf_op jit(solution)/shard_map/reduce_scatter | solution.py:104
  397.9 1.1 convert_element_type.26
  399.0 1.2 convolution_bitcast_fusion.1
  400.2 0.8 copy.52
  401.0 146.5 %all-reduce.3.cloned.1.call-done = (f32[256,256]{0,1:T(8,128)}, f32[256,256]{0,1:T(8,128)}) async-done(((f32[256,256]{0,1:T(8,128)}, f32[256,256]{0,1:T(8,128)}), (f32[256,256]{0,1:T(8,128)}, f32[256,256]{0,1:T(8,128)})) %all-reduce.3.cloned.1.call-update) | async-done | bytes 524304 | tf_op jit(solution)/shard_map/psum | solution.py:114
  547.5 1.0 broadcast_multiply_fusion.2
  548.5 0.8 copy.53
  549.3 1.0 broadcast_multiply_fusion.1
  550.3 0.8 copy.54
  (50 shorter events, 1.4 us)
Async XLA Ops:
  7.2 1.0 copy-start
  7.2 5.9 %copy-start.6 = (s32[512]{0:T(512)S(1)}, s32[512]{0:T(512)}, u32[]{:S(2)}) copy-start(s32[512]{0:T(512)} %param.16) | copy-start | bytes 6148
  7.2 4.9 copy-start.3
  12.3 5.4 copy-start.4
  17.0 0.7 copy-start.1
  20.4 61.2 %all-to-all-start = ((bf16[16,512,256]{2,1,0:T(8,128)(2,1)}), bf16[16,512,256]{2,1,0:T(8,128)(2,1)}, u32[]{:S(2)}, u32[]{:S(2)}) async-start(bf16[16,512,256]{2,1,0:T(8,128)(2,1)} %stack.2), calls=%async_computation | async-start | bytes 8388608 | tf_op jit(solution)/shard_map/all_to_all | solution.py:60
  28.8 369.0 %reduce-scatter.2.cloned.1.call-start = ((), (), s32[]{:S(2)}) async-start(), calls=%async_computation.2 | async-start | bytes 4718592 | tf_op jit(solution)/shard_map/reduce_scatter | solution.py:104
  28.9 27.9 %copy-start.7 = (s32[1,16,2]{1,2,0:T(2,128)S(1)}, s32[1,16,2]{1,2,0:T(2,128)}, u32[]{:S(2)}) copy-start(s32[1,16,2]{1,2,0:T(2,128)} %param.23) | copy-start | bytes 388
  28.9 28.7 %copy-start.5 = (s32[640]{0:T(1024)S(1)}, s32[640]{0:T(1024)}, u32[]{:S(2)}) copy-start(s32[640]{0:T(1024)} %param.20) | copy-start | bytes 7684
  328.6 8.1 %copy-start.2 = (bf16[512,256]{0,1:T(8,128)(2,1)S(1)}, bf16[512,256]{0,1:T(8,128)(2,1)}, u32[]{:S(2)}) copy-start(bf16[512,256]{0,1:T(8,128)(2,1)} %copy-done.1) | copy-start | bytes 786436
  328.6 70.4 %copy-start.8 = (bf16[512,256]{1,0:T(8,128)(2,1)S(1)}, bf16[512,256]{1,0:T(8,128)(2,1)}, u32[]{:S(2)}) copy-start(bf16[512,256]{1,0:T(8,128)(2,1)} %param.13) | copy-start | bytes 786436
  328.6 70.4 %copy-start.9 = (bf16[256,256]{1,0:T(8,128)(2,1)S(1)}, bf16[256,256]{1,0:T(8,128)(2,1)}, u32[]{:S(2)}) copy-start(bf16[256,256]{1,0:T(8,128)(2,1)} %param.17) | copy-start | bytes 393220
  336.6 210.9 %all-reduce.3.cloned.1.call-start = ((), (), s32[]{:S(2)}) async-start(), calls=%async_computation.3 | async-start | bytes 1048576 | tf_op jit(solution)/shard_map/psum | solution.py:114
Sparse Core Ops, SparseCore 0:
  336.8 61.0 reduce-scatter.1
  403.4 144.0 all-reduce.2
